TPU v7x, 512 devices: a whole 4x8x8 slice. The times are simulated.
512 devices in a mesh: gx: 32 (over y, x), gy: 16 (over z, core).
Axes of the slice: x: 4, y: 8, z: 8, core: 2. Of those that a mesh axis runs over, the one named last changes fastest.
Arguments:
- hidden_in: bfloat16 [4096, 2560], P('gx'), may hold values from -48 to 48
- norm_gain: bfloat16 [2560], replicated, may hold values from 0.099609375 to 1.8984375
- router_weight: bfloat16 [2560, 64], replicated, may hold values from -3 to 3
- routes: int32 [4096, 6], P('gx'), may hold values from 0 to 63, as said below
- w_gate_up: bfloat16 [512, 2560, 384], P(('gx', 'gy')), may hold values from -0.125 to 0.125
- w_down: bfloat16 [512, 192, 2560], P(('gx', 'gy')), may hold values from -0.15625 to 0.15625
- final_gain: bfloat16 [2560], replicated, may hold values from 0.099609375 to 1.8984375
- head_weight: bfloat16 [2560, 53248], P('gy', 'gx'), may hold values from -5 to 5
- targets: int32 [4096], replicated, may hold values from 0 to 53247
Outputs:
- logprob: float32 [32, 128], P(None, 'gy')
- entropy: float32 [32, 128], P(None, 'gy')
Inputs may be any that keep to these rules, and one draw needn't show every extreme that they name: `routes`: each row names 6 different experts. Within the 128 rows of one index of gx no expert is named by more than 16 rows, and one expert, the same for every index of gx, is named by exactly 16 rows in each.
All inputs are finite; a program needn't handle non-finite values.
Results may differ from a plain program's by a relative error of at most 0.012.
Values may be sent and summed in bfloat16 or wider, within the bound.
A program may use at most 192 MiB of HBM per device.

v0:
```python
import jax
import jax.numpy as jnp
from jax import lax
from jax.sharding import PartitionSpec as P

SPLITS = 8
NORM_EPSILON = 1e-06


def rms_scale(values, gain_vector):
    widened = values.astype(jnp.float32)
    return (
        widened
        * lax.rsqrt(jnp.mean(widened * widened, -1, keepdims=True) + NORM_EPSILON)
        * gain_vector.astype(jnp.float32)
    )


def finish(peak_value, total_mass, spread, target_logit):
    log_mass = jnp.log(total_mass)
    return (target_logit - peak_value - log_mass, log_mass - spread / total_mass)


def shards(
    hidden_in, norm_gain, router_weight, routes, w_gate_up, w_down, final_gain, head_weight, targets
):
    tok_rows = hidden_in.shape[0]
    group_count = lax.axis_size("gx")
    lane_count = lax.axis_size("gy")
    group_index = lax.axis_index("gx")
    lane_index = lax.axis_index("gy")
    expert_count = router_weight.shape[1]
    held_slices = w_gate_up.shape[0]
    unit_count = w_down.shape[1]
    slot_count = tok_rows // 8
    share_rows = tok_rows // lane_count
    columns = head_weight.shape[1]
    normed = rms_scale(hidden_in, norm_gain).astype(jnp.bfloat16)
    scores = jnp.dot(normed, router_weight, preferred_element_type=jnp.float32)
    chosen = routes[:, :, None] == jnp.arange(expert_count, dtype=jnp.int32)[None, None, :]
    picked = jnp.sum(jnp.where(chosen, scores[:, None, :], 0.0), -1)
    gate_values = jax.nn.softmax(picked, axis=-1).astype(jnp.bfloat16)
    gate_table = jnp.sum(jnp.where(chosen, gate_values.astype(jnp.float32)[:, :, None], 0.0), 1)
    member = jnp.sum(chosen.astype(jnp.int32), 1)
    slot_rank = jnp.cumsum(member, 0) - member
    slot_hit = (member[:, :, None] == 1) & (
        slot_rank[:, :, None] == jnp.arange(slot_count, dtype=jnp.int32)[None, None, :]
    )
    lane_slices = (
        jnp.arange(group_count, dtype=jnp.int32)[:, None] * lane_count + lane_index
    ) * held_slices + jnp.arange(held_slices, dtype=jnp.int32)[None, :]
    owner_expert = lane_slices // SPLITS
    pick_expert = (
        owner_expert[:, :, None] == jnp.arange(expert_count, dtype=jnp.int32)[None, None, :]
    ).astype(jnp.bfloat16)
    dispatch = jnp.einsum(
        "tke,nec->tkcn",
        pick_expert,
        slot_hit.astype(jnp.bfloat16),
        preferred_element_type=jnp.float32,
    ).astype(jnp.bfloat16)
    outgoing = jnp.einsum(
        "tkcn,nd->tkcd", dispatch, normed, preferred_element_type=jnp.float32
    ).astype(jnp.bfloat16)
    expert_gate = jnp.einsum(
        "tke,ne->tkn",
        pick_expert,
        gate_table.astype(jnp.bfloat16),
        preferred_element_type=jnp.float32,
    )
    combine = (dispatch.astype(jnp.float32) * expert_gate[:, :, None, :]).astype(jnp.bfloat16)
    lifted = jnp.einsum(
        "skcd,kdf->skcf",
        lax.all_to_all(outgoing, "gx", split_axis=0, concat_axis=0, tiled=True),
        w_gate_up,
        preferred_element_type=jnp.float32,
    )
    active = (jax.nn.silu(lifted[..., :unit_count]) * lifted[..., unit_count:]).astype(jnp.bfloat16)
    result = jnp.einsum(
        "skcf,kfd->skcd", active, w_down, preferred_element_type=jnp.float32
    ).astype(jnp.bfloat16)
    returned = lax.all_to_all(result, "gx", split_axis=0, concat_axis=0, tiled=True)
    partial_value = jnp.einsum(
        "tkcn,tkcd->nd", combine, returned, preferred_element_type=jnp.float32
    )
    summed = lax.psum_scatter(partial_value, "gy", scatter_dimension=0, tiled=True)
    residual = lax.dynamic_slice_in_dim(hidden_in, lane_index * share_rows, share_rows, 0)
    layer_out = (residual.astype(jnp.float32) + summed).astype(jnp.bfloat16)
    final_states = rms_scale(layer_out, final_gain).astype(jnp.bfloat16)
    gathered = lax.all_gather(final_states, "gx", axis=0, tiled=True)
    target_grid = targets.reshape(group_count, tok_rows)
    logits = jnp.dot(
        gathered,
        lax.all_gather(head_weight, "gy", axis=0, tiled=True),
        preferred_element_type=jnp.float32,
    )
    offset = group_index * columns
    own_targets = lax.dynamic_slice_in_dim(
        target_grid, lane_index * share_rows, share_rows, 1
    ).reshape(group_count * share_rows)
    target_hits = (offset + jnp.arange(columns, dtype=jnp.int32))[None, :] == own_targets[:, None]
    peak_value = lax.pmax(jnp.max(logits, -1), "gx")
    shifted = logits - peak_value[:, None]
    weights = jnp.exp(shifted)
    total_mass, spread, target_logit = lax.psum(
        (
            jnp.sum(weights, -1),
            jnp.sum(weights * shifted, -1),
            jnp.sum(jnp.where(target_hits, logits, 0.0), -1),
        ),
        "gx",
    )
    logprob, entropy = finish(peak_value, total_mass, spread, target_logit)
    return (logprob.reshape(group_count, share_rows), entropy.reshape(group_count, share_rows))


def solution(mesh):
    return jax.shard_map(
        shards,
        mesh=mesh,
        in_specs=(
            P("gx", None),
            P(),
            P(),
            P("gx", None),
            P(("gx", "gy"), None, None),
            P(("gx", "gy"), None, None),
            P(),
            P("gy", "gx"),
            P(),
        ),
        out_specs=(P(None, "gy"), P(None, "gy")),
        check_vma=False,
    )
```

profile of v0, /device:TPU:2, one launch (start us, length us, event | category | flops | bytes accessed | tf_op | source)
XLA Modules:
  0.0 525.7 jit_solution(14808827266614481248)
XLA Ops:
  7.2 0.0 copy-start
  7.2 0.0 copy-start.1
  7.2 0.9 convert_reduce_fusion
  8.1 0.1 copy.35
  8.2 0.7 convert_element_type.89
  8.9 1.3 fusion.8
  10.2 0.2 reduce_window_sum.11
  10.4 0.1 copy.37
  10.4 0.3 convolution_convert_fusion.2
  10.7 0.0 copy-done.1
  10.7 0.9 fusion.1
  11.7 71.8 %all_to_all.10 = bf16[32,1,16,2560]{3,2,1,0:T(8,128)(2,1)S(1)} all-to-all(bf16[32,1,16,2560]{3,2,1,0:T(8,128)(2,1)S(1)} %fusion.1), channel_id=1, replica_groups=mesh['gx'=32,'gy'=16] {'gx'}, dimensions={0} | all-to-all | bytes 5242880 | tf_op jit(solution)/shard_map/all_to_all | solution.py:74
  83.5 0.0 copy-done
  83.5 0.0 copy-start.5
  83.5 1.5 fusion.11
  85.0 0.0 copy-done.5
  85.0 2.4 fusion
  87.5 0.0 copy-start.6
  87.5 0.0 copy-start.2
  87.5 5.8 %all-to-all-start.1 = ((bf16[32,1,16,2560]{3,2,1,0:T(8,128)(2,1)}), bf16[32,1,16,2560]{3,2,1,0:T(8,128)(2,1)}, u32[]{:S(2)}, u32[]{:S(2)}) async-start(bf16[32,1,16,2560]{3,2,1,0:T(8,128)(2,1)} %fusion), calls=%async_computation.1 | async-start | bytes 5242880 | tf_op jit(solution)/shard_map/all_to_all | solution.py:82
  93.3 0.0 reduce-scatter.2.cloned.1.call-start
  93.3 0.0 copy-done.6
  93.3 0.4 fusion.26
  93.8 0.0 copy-done.2
  93.9 0.2 fusion.36
  94.1 0.0 copy-start.4
  94.1 58.5 %all-to-all-done.1 = bf16[32,1,16,2560]{3,2,1,0:T(8,128)(2,1)} async-done(((bf16[32,1,16,2560]{3,2,1,0:T(8,128)(2,1)}), bf16[32,1,16,2560]{3,2,1,0:T(8,128)(2,1)}, u32[]{:S(2)}, u32[]{:S(2)}) %all-to-all-start.1) | async-done | bytes 2621472 | tf_op jit(solution)/shard_map/all_to_all | solution.py:82
  152.6 4.5 convolution_bitcast_fusion
  157.1 0.0 copy-start.3
  157.1 0.0 reduce-scatter.2.cloned.1.call-update
  157.1 0.0 all-gather.3.cloned.1.call-start
  157.2 0.0 copy-done.4
  157.2 62.9 %reduce-scatter.2.cloned.1.call-done = f32[8,2560]{1,0:T(8,128)} async-done(((f32[128,2560]{1,0:T(8,128)}), f32[8,2560]{1,0:T(8,128)}) %reduce-scatter.2.cloned.1.call-update) | async-done | bytes 81936 | tf_op jit(solution)/shard_map/reduce_scatter | solution.py:86
  220.1 1.0 fusion.33
  221.1 0.7 fusion.35
  221.8 0.0 all-gather.3.cloned.1.call-update
  221.8 0.0 all-gather.5.cloned.1.call-start
  221.9 0.7 all-gather.5.cloned.1.call-update
  222.6 0.0 copy-done.3
  222.6 0.1 constant_dynamic-slice_fusion
  222.7 0.1 eq.70
  222.8 79.2 %all-gather.3.cloned.1.call-done = bf16[256,2560]{1,0:T(8,128)(2,1)} async-done(((bf16[8,2560]{1,0:T(8,128)(2,1)}), bf16[256,2560]{1,0:T(8,128)(2,1)}) %all-gather.3.cloned.1.call-update) | async-done | bytes 1310736 | tf_op jit(solution)/shard_map/all_gather | solution.py:90
  301.9 61.2 %all-gather.5.cloned.1.call-done = bf16[2560,1664]{1,0:T(8,128)(2,1)} async-done(((bf16[160,1664]{1,0:T(8,128)(2,1)}), bf16[2560,1664]{1,0:T(8,128)(2,1)}) %all-gather.5.cloned.1.call-update) | async-done | bytes 8519696 | tf_op jit(solution)/shard_map/all_gather | solution.py:94
  363.1 7.6 %fusion.45 = (f32[256]{0:T(256)S(1)}, f32[256,1664]{1,0:T(8,128)}) fusion(bf16[256,2560]{1,0:T(8,128)(2,1)} %all-gather.3.cloned.1.call-done, bf16[2560,1664]{1,0:T(8,128)(2,1)} %all-gather.5.cloned.1.call-done), kind=kOutput, calls=%fused_computation.68 | convolution fusion | flops 2181463808 | bytes 11535360 | tf_op jit(solution)/shard_map/dot_general | solution.py:92
  370.7 70.6 %pmax.7 = f32[256]{0:T(256)S(1)} all-reduce(f32[256]{0:T(256)S(1)} %get-tuple-element.18), channel_id=1, replica_groups=mesh['gx'=32,'gy'=16] {'gx'}, use_global_device_ids=true, to_apply=%region_12.13 | all-reduce | flops 256 | bytes 2048 | tf_op jit(solution)/shard_map/pmax | solution.py:102
  441.4 2.1 fusion.7
  443.5 74.1 %all-reduce = (f32[256]{0:T(256)S(1)}, f32[256]{0:T(256)S(1)}, f32[256]{0:T(256)S(1)}) all-reduce(f32[256]{0:T(256)S(1)} %get-tuple-element.10, f32[256]{0:T(256)S(1)} %get-tuple-element.9, f32[256]{0:T(256)S(1)} %get-tuple-element.8), channel_id=1, replica_groups=mesh['gx'=32,'gy'=16] {'gx'}, use_global_device_ids=true, to_apply=%region_10.11 | all-reduce | flops 768 | bytes 6144 | tf_op jit(solution)/shard_map/psum | solution.py:105
  517.6 0.1 reshape.187
  517.7 0.7 copy.42
  518.4 0.1 reshape.188
  518.5 0.7 copy.43
  (13 shorter events, 0.2 us)
Async XLA Ops:
  7.2 76.3 %copy-start = (bf16[1,2560,384]{2,1,0:T(8,128)(2,1)S(1)}, bf16[1,2560,384]{2,1,0:T(8,128)(2,1)}, u32[]{:S(2)}) copy-start(bf16[1,2560,384]{2,1,0:T(8,128)(2,1)} %param.13) | copy-start | bytes 5898244
  7.2 3.5 copy-start.1
  83.5 1.5 copy-start.5
  87.5 5.8 %copy-start.6 = (bf16[2560,64]{0,1:T(8,128)(2,1)S(1)}, bf16[2560,64]{0,1:T(8,128)(2,1)}, u32[]{:S(2)}) copy-start(bf16[2560,64]{0,1:T(8,128)(2,1)} %param.11) | copy-start | bytes 983044
  87.5 6.3 %copy-start.2 = (s32[128,6]{0,1:T(8,128)S(1)}, s32[128,6]{0,1:T(8,128)}, u32[]{:S(2)}) copy-start(s32[128,6]{0,1:T(8,128)} %param.12) | copy-start | bytes 9220
  87.5 65.1 %all-to-all-start.1 = ((bf16[32,1,16,2560]{3,2,1,0:T(8,128)(2,1)}), bf16[32,1,16,2560]{3,2,1,0:T(8,128)(2,1)}, u32[]{:S(2)}, u32[]{:S(2)}) async-start(bf16[32,1,16,2560]{3,2,1,0:T(8,128)(2,1)} %fusion), calls=%async_computation.1 | async-start | bytes 5242880 | tf_op jit(solution)/shard_map/all_to_all | solution.py:82
  93.3 126.8 %reduce-scatter.2.cloned.1.call-start = ((), (), s32[]{:S(2)}) async-start(), calls=%async_computation.3 | async-start | bytes 1392640 | tf_op jit(solution)/shard_map/reduce_scatter | solution.py:86
  94.1 63.1 %copy-start.4 = (bf16[2560]{0:T(1024)(128)(2,1)S(1)}, bf16[2560]{0:T(1024)(128)(2,1)}, u32[]{:S(2)}) copy-start(bf16[2560]{0:T(1024)(128)(2,1)} %param.15) | copy-start | bytes 15364
  157.1 65.5 %copy-start.3 = (s32[4096]{0:T(1024)S(1)}, s32[4096]{0:T(1024)}, u32[]{:S(2)}) copy-start(s32[4096]{0:T(1024)} %param.17) | copy-start | bytes 49156
  157.1 144.8 %all-gather.3.cloned.1.call-start = ((), (), s32[]{:S(2)}) async-start(), calls=%async_computation.4 | async-start | bytes 1351680 | tf_op jit(solution)/shard_map/all_gather | solution.py:90
  221.8 141.3 %all-gather.5.cloned.1.call-start = ((), (), s32[]{:S(2)}) async-start(), calls=%async_computation.5 | async-start | bytes 9052160 | tf_op jit(solution)/shard_map/all_gather | solution.py:94
Sparse Core Ops, SparseCore 0:
  157.2 62.7 reduce-scatter.1
  223.2 78.6 all-gather.2
  304.1 59.0 all-gather.4
where the time goes:
time: 526 us
  waiting for transfers between devices  262 us (50%)
  blocking collectives  217 us (41%)
  matrix products  17.9 us (3%)
  between operations  13.9 us (3%)
  other arithmetic  7.05 us (1%)
  starting transfers between devices  5.9 us (1%)
    all_gather x1, waiting for transfers between devices, shards(): gathered = lax.all_gather(final_states, 'gx', axis=0, tiled=True)  79.2 us
    psum x1, blocking collectives, shards(): lax.psum((jnp.sum(weights, -1), jnp.sum(weights * shifted, -1), jnp.sum(j...  74.1 us
    all_to_all x1, blocking collectives, shards(): lax.all_to_all(outgoing, 'gx', split_axis=0, concat_axis=0, tiled=True)  71.8 us
    pmax x1, blocking collectives, shards(): peak_value = lax.pmax(jnp.max(logits, -1), 'gx')  70.6 us
    reduce_scatter x1, waiting for transfers between devices, shards(): lax.psum_scatter(partial_value, 'gy', scatter_dimension=0, tiled=True)  62.9 us
    all_gather x1, waiting for transfers between devices, shards(): lax.all_gather(head_weight, 'gy', axis=0, tiled=True)  61.2 us
    all_to_all x1, waiting for transfers between devices, shards(): lax.all_to_all(result, 'gx', split_axis=0, concat_axis=0, tiled=True)  58.5 us
  transfers between devices with their start and end apart: 4, of which 4 were waited for; matrix products, arithmetic and copies ran while one was open for 0% of the time, Pallas kernels for 0%

commit v1 on v0

--- a/solution.py
+++ b/solution.py
@@ -5,6 +5,19 @@
 
 SPLITS = 8
 NORM_EPSILON = 1e-06
+
+
+def gather_around(value, axis, dim):
+    ways = lax.axis_size(axis)
+    up = [(d, (d + 1) % ways) for d in range(ways)]
+    down = [(d, (d - 1) % ways) for d in range(ways)]
+    earlier, later = ([value], [value])
+    for _ in range(ways // 2):
+        earlier.append(lax.ppermute(earlier[-1], axis, up))
+    for _ in range((ways - 1) // 2):
+        later.append(lax.ppermute(later[-1], axis, down))
+    line = jnp.concatenate([*earlier[::-1], *later[1:]], axis=dim)
+    return jnp.roll(line, (lax.axis_index(axis) - ways // 2) * value.shape[dim], axis=dim)
 
 
 def rms_scale(values, gain_vector):
@@ -90,9 +103,7 @@
     gathered = lax.all_gather(final_states, "gx", axis=0, tiled=True)
     target_grid = targets.reshape(group_count, tok_rows)
     logits = jnp.dot(
-        gathered,
-        lax.all_gather(head_weight, "gy", axis=0, tiled=True),
-        preferred_element_type=jnp.float32,
+        gathered, gather_around(head_weight, "gy", 0), preferred_element_type=jnp.float32
     )
     offset = group_index * columns
     own_targets = lax.dynamic_slice_in_dim(

time: 526 us -> 474 us (0.901)
  waiting for transfers between devices: 262 us -> 177 us
  blocking collectives: 217 us -> 143 us
  local copies, waits for them, and re-layouts: 1.86 us -> 61.7 us
  starting transfers between devices: 5.9 us -> 44.4 us
  matrix products: 17.9 us -> 24.4 us
    all_to_all x1 -> x0, blocking collectives: 71.8 us -> none  [shards(): lax.all_to_all(outgoing, 'gx', split_axis=0, concat_axis=0, tiled=True)]
    all_gather x1 -> x0, waiting for transfers between devices: 61.2 us -> none  [shards(): lax.all_gather(head_weight, 'gy', axis=0, tiled=True)]
    all_to_all x1, waiting for transfers between devices: 58.5 us -> 0.01 us  [shards(): lax.all_to_all(result, 'gx', split_axis=0, concat_axis=0, tiled=True)]
    unnamed x16 -> x51, local copies, waits for them, and re-layouts: 1.38 us -> 59.4 us
    ppermute x0 -> x15, waiting for transfers between devices: none -> 55.6 us  [the longest x8 29.1 us: gather_around(): earlier.append(lax.ppermute(earlier[-1], axis, up))]
    ppermute x0 -> x15, starting transfers between devices: none -> 26.7 us  [the longest x7 26.7 us: gather_around(): later.append(lax.ppermute(later[-1], axis, down))]
    reduce_scatter x1, waiting for transfers between devices: 62.9 us -> 37.6 us  [shards(): lax.psum_scatter(partial_value, 'gy', scatter_dimension=0, tiled=True)]
    all_to_all x0 -> x1, waiting for transfers between devices: none -> 23.5 us  [shards(): lax.all_to_all(outgoing, 'gx', split_axis=0, concat_axis=0, tiled=True)]
  transfers between devices with their start and end apart: 4 -> 19, of which waited for: 4 -> 10; matrix products, arithmetic and copies ran while one was open for 0% -> 15% of each run, Pallas kernels for 0% -> 0%
where the time goes in v1:
time: 474 us; the launch traced here: 472 us
  waiting for transfers between devices  177 us (37%)
  blocking collectives  143 us (30%)
  local copies, waits for them, and re-layouts  61.7 us (13%)
  starting transfers between devices  44.4 us (9%)
  matrix products  24.4 us (5%)
  between operations  14.3 us (3%)
  other arithmetic  7.03 us (1%)
    psum x1, blocking collectives, shards(): lax.psum((jnp.sum(weights, -1), jnp.sum(weights * shifted, -1), jnp.sum(j...  72.1 us
    pmax x1, blocking collectives, shards(): peak_value = lax.pmax(jnp.max(logits, -1), 'gx')  71.3 us
    all_gather x1, waiting for transfers between devices, shards(): gathered = lax.all_gather(final_states, 'gx', axis=0, tiled=True)  60.3 us
    unnamed x51, local copies, waits for them, and re-layouts  59.4 us
    reduce_scatter x1, waiting for transfers between devices, shards(): lax.psum_scatter(partial_value, 'gy', scatter_dimension=0, tiled=True)  37.6 us
    ppermute x8, waiting for transfers between devices, gather_around(): earlier.append(lax.ppermute(earlier[-1], axis, up))  29.1 us
    ppermute x7, starting transfers between devices, gather_around(): later.append(lax.ppermute(later[-1], axis, down))  26.7 us
    ppermute x7, waiting for transfers between devices, gather_around(): later.append(lax.ppermute(later[-1], axis, down))  26.4 us
  transfers between devices with their start and end apart: 19, of which 10 were waited for; matrix products, arithmetic and copies ran while one was open for 15% of the time, Pallas kernels for 0%

profile of v1, /device:TPU:2, one launch (start us, length us, event | category | flops | bytes accessed | tf_op | source)
XLA Modules:
  0.0 472.2 jit_solution(8768627438559697953)
XLA Ops:
  7.2 0.9 convert_reduce_fusion
  8.9 1.3 fusion.10
  10.7 3.6 fusion.3
  14.3 10.3 %all-to-all-start = ((bf16[32,1,16,2560]{3,2,1,0:T(8,128)(2,1)}), bf16[32,1,16,2560]{3,2,1,0:T(8,128)(2,1)}, u32[]{:S(2)}, u32[]{:S(2)}) async-start(bf16[32,1,16,2560]{3,2,1,0:T(8,128)(2,1)} %fusion.3), calls=%async_computation | async-start | bytes 5242880 | tf_op jit(solution)/shard_map/all_to_all | solution.py:87
  24.6 15.1 %collective-permute-done = bf16[160,1664]{1,0:T(8,128)(2,1)S(1)} collective-permute-done((bf16[160,1664]{1,0:T(8,128)(2,1)}, bf16[160,1664]{1,0:T(8,128)(2,1)S(1)}, u32[]{:S(2)}, u32[]{:S(2)}) %collective-permute-start) | collective-permute-done | bytes 532512 | tf_op jit(solution)/shard_map/ppermute | solution.py:16
  40.6 3.0 collective-permute-start.8
  43.5 6.9 %collective-permute-done.1 = bf16[160,1664]{1,0:T(8,128)(2,1)S(1)} collective-permute-done((bf16[160,1664]{1,0:T(8,128)(2,1)S(1)}, bf16[160,1664]{1,0:T(8,128)(2,1)S(1)}, u32[]{:S(2)}, u32[]{:S(2)}) %collective-permute-start.1) | collective-permute-done | bytes 532512 | tf_op jit(solution)/shard_map/ppermute | solution.py:16
  51.3 3.0 collective-permute-start.9
  54.2 7.0 %collective-permute-done.2 = bf16[160,1664]{1,0:T(8,128)(2,1)} collective-permute-done((bf16[160,1664]{1,0:T(8,128)(2,1)S(1)}, bf16[160,1664]{1,0:T(8,128)(2,1)}, u32[]{:S(2)}, u32[]{:S(2)}) %collective-permute-start.2) | collective-permute-done | bytes 532512 | tf_op jit(solution)/shard_map/ppermute | solution.py:16
  61.3 23.5 %all-to-all-done = bf16[32,1,16,2560]{3,2,1,0:T(8,128)(2,1)} async-done(((bf16[32,1,16,2560]{3,2,1,0:T(8,128)(2,1)}), bf16[32,1,16,2560]{3,2,1,0:T(8,128)(2,1)}, u32[]{:S(2)}, u32[]{:S(2)}) %all-to-all-start) | async-done | bytes 2621472 | tf_op jit(solution)/shard_map/all_to_all | solution.py:87
  84.7 3.2 fusion.13
  88.0 3.6 fusion.2
  91.6 7.3 %all-to-all-start.1 = ((bf16[32,1,16,2560]{3,2,1,0:T(8,128)(2,1)}), bf16[32,1,16,2560]{3,2,1,0:T(8,128)(2,1)}, u32[]{:S(2)}, u32[]{:S(2)}) async-start(bf16[32,1,16,2560]{3,2,1,0:T(8,128)(2,1)} %fusion.2), calls=%async_computation.1 | async-start | bytes 5242880 | tf_op jit(solution)/shard_map/all_to_all | solution.py:95
  99.0 7.1 %collective-permute-start.10 = (bf16[160,1664]{1,0:T(8,128)(2,1)}, bf16[160,1664]{1,0:T(8,128)(2,1)}, u32[]{:S(2)}, u32[]{:S(2)}) collective-permute-start(bf16[160,1664]{1,0:T(8,128)(2,1)} %collective-permute-done.9), channel_id=1, source_target_pairs={{0,15},{1,0},{2,1},{3,2},{4,3},{5,4},{6,5},{7,6},{8,7},{9,8},{10,9... | collective-permute-start | bytes 1597448 | tf_op jit(solution)/shard_map/ppermute | solution.py:18
  106.1 7.1 %collective-permute-done.10 = bf16[160,1664]{1,0:T(8,128)(2,1)} collective-permute-done((bf16[160,1664]{1,0:T(8,128)(2,1)}, bf16[160,1664]{1,0:T(8,128)(2,1)}, u32[]{:S(2)}, u32[]{:S(2)}) %collective-permute-start.10) | collective-permute-done | bytes 532512 | tf_op jit(solution)/shard_map/ppermute | solution.py:18
  113.2 3.4 collective-permute-start.11
  116.8 6.9 %collective-permute-done.11 = bf16[160,1664]{1,0:T(8,128)(2,1)} collective-permute-done((bf16[160,1664]{1,0:T(8,128)(2,1)}, bf16[160,1664]{1,0:T(8,128)(2,1)}, u32[]{:S(2)}, u32[]{:S(2)}) %collective-permute-start.11) | collective-permute-done | bytes 532512 | tf_op jit(solution)/shard_map/ppermute | solution.py:18
  123.7 3.4 collective-permute-start.12
  127.1 1.4 fusion.28
  128.6 5.6 %collective-permute-done.12 = bf16[160,1664]{1,0:T(8,128)(2,1)} collective-permute-done((bf16[160,1664]{1,0:T(8,128)(2,1)}, bf16[160,1664]{1,0:T(8,128)(2,1)}, u32[]{:S(2)}, u32[]{:S(2)}) %collective-permute-start.12) | collective-permute-done | bytes 532512 | tf_op jit(solution)/shard_map/ppermute | solution.py:18
  134.2 3.4 collective-permute-start.13
  137.9 6.9 %collective-permute-done.13 = bf16[160,1664]{1,0:T(8,128)(2,1)} collective-permute-done((bf16[160,1664]{1,0:T(8,128)(2,1)}, bf16[160,1664]{1,0:T(8,128)(2,1)}, u32[]{:S(2)}, u32[]{:S(2)}) %collective-permute-start.13) | collective-permute-done | bytes 532512 | tf_op jit(solution)/shard_map/ppermute | solution.py:18
  144.8 3.4 collective-permute-start.14
  148.2 0.9 copy-done.5
  149.0 0.8 constant_dynamic-update-slice_fusion.31
  149.9 1.9 constant_dynamic-update-slice_fusion.30
  151.8 1.9 constant_dynamic-update-slice_fusion.29
  153.7 1.9 constant_dynamic-update-slice_fusion.28
  155.5 1.9 constant_dynamic-update-slice_fusion.27
  157.4 1.9 constant_dynamic-update-slice_fusion.26
  159.3 1.9 constant_dynamic-update-slice_fusion.25
  161.2 1.9 constant_dynamic-update-slice_fusion.24
  163.1 0.9 constant_dynamic-update-slice_fusion.23
  163.9 1.9 constant_dynamic-update-slice_fusion.22
  165.8 4.5 convolution_bitcast_fusion
  170.4 1.9 constant_dynamic-update-slice_fusion.21
  172.3 1.9 constant_dynamic-update-slice_fusion.20
  174.2 1.9 constant_dynamic-update-slice_fusion.19
  176.1 1.9 constant_dynamic-update-slice_fusion.18
  178.0 1.9 constant_dynamic-update-slice_fusion.17
  179.8 1.9 constant_dynamic-update-slice_fusion.16
  181.7 1.9 constant_dynamic-update-slice_fusion.15
  183.7 1.9 constant_dynamic-update-slice_fusion.14
  185.6 1.9 constant_dynamic-update-slice_fusion.13
  187.5 1.9 constant_dynamic-update-slice_fusion.12
  189.4 1.9 constant_dynamic-update-slice_fusion.11
  191.3 37.6 %reduce-scatter.2.cloned.1.call-done = f32[8,2560]{1,0:T(8,128)} async-done(((f32[128,2560]{1,0:T(8,128)}), f32[8,2560]{1,0:T(8,128)}) %reduce-scatter.2.cloned.1.call-update) | async-done | bytes 81936 | tf_op jit(solution)/shard_map/reduce_scatter | solution.py:99
  228.8 1.0 fusion.35
  230.6 1.9 constant_dynamic-update-slice_fusion.10
  232.4 1.9 constant_dynamic-update-slice_fusion.9
  234.3 1.9 constant_dynamic-update-slice_fusion.8
  236.2 0.9 constant_dynamic-update-slice_fusion.7
  237.1 1.9 constant_dynamic-update-slice_fusion.6
  239.0 1.9 constant_dynamic-update-slice_fusion.5
  240.9 1.9 constant_dynamic-update-slice_fusion.4
  242.7 1.9 constant_dynamic-update-slice_fusion.3
  244.6 1.9 constant_dynamic-update-slice_fusion.2
  246.5 1.9 constant_dynamic-update-slice_fusion.1
  248.4 1.9 constant_dynamic-update-slice_fusion
  250.3 60.3 %all-gather.2.cloned.1.call-done = bf16[256,2560]{1,0:T(8,128)(2,1)} async-done(((bf16[8,2560]{1,0:T(8,128)(2,1)}), bf16[256,2560]{1,0:T(8,128)(2,1)}) %all-gather.2.cloned.1.call-update) | async-done | bytes 1310736 | tf_op jit(solution)/shard_map/all_gather | solution.py:103
  310.7 7.6 %fusion.48 = (f32[256]{0:T(256)S(1)}, f32[256,1664]{1,0:T(8,128)}) fusion(bf16[256,2560]{1,0:T(8,128)(2,1)} %all-gather.2.cloned.1.call-done, bf16[5120,1664]{1,0:T(8,128)(2,1)} %constant_dynamic-update-slice_fusion, s32[]{:T(128)S(6)} %select_n.45), kind=kOutput, calls=%fused_computation.103 | convolution fusion | flops 2181463808 | bytes 11535364 | tf_op jit(solution)/shard_map/dot_general | solution.py:105
  318.3 71.3 %pmax.7 = f32[256]{0:T(256)S(1)} all-reduce(f32[256]{0:T(256)S(1)} %get-tuple-element.18), channel_id=1, replica_groups=mesh['gx'=32,'gy'=16] {'gx'}, use_global_device_ids=true, to_apply=%region_12.13 | all-reduce | flops 256 | bytes 2048 | tf_op jit(solution)/shard_map/pmax | solution.py:113
  389.6 2.1 fusion.9
  391.8 72.1 %all-reduce = (f32[256]{0:T(256)S(1)}, f32[256]{0:T(256)S(1)}, f32[256]{0:T(256)S(1)}) all-reduce(f32[256]{0:T(256)S(1)} %get-tuple-element.10, f32[256]{0:T(256)S(1)} %get-tuple-element.9, f32[256]{0:T(256)S(1)} %get-tuple-element.8), channel_id=1, replica_groups=mesh['gx'=32,'gy'=16] {'gx'}, use_global_device_ids=true, to_apply=%region_10.11 | all-reduce | flops 768 | bytes 6144 | tf_op jit(solution)/shard_map/psum | solution.py:116
  (64 shorter events, 5.8 us)
Async XLA Ops:
  7.2 77.6 %copy-start = (bf16[1,2560,384]{2,1,0:T(8,128)(2,1)S(1)}, bf16[1,2560,384]{2,1,0:T(8,128)(2,1)}, u32[]{:S(2)}) copy-start(bf16[1,2560,384]{2,1,0:T(8,128)(2,1)} %param.13) | copy-start | bytes 5898244
  7.2 120.0 %copy-start.1 = (bf16[128,2560]{1,0:T(8,128)(2,1)S(1)}, bf16[128,2560]{1,0:T(8,128)(2,1)}, u32[]{:S(2)}) copy-start(bf16[128,2560]{1,0:T(8,128)(2,1)} %param.9) | copy-start | bytes 1966084
  7.2 109.4 %copy-start.8 = (bf16[2560]{0:T(1024)(128)(2,1)S(1)}, bf16[2560]{0:T(1024)(128)(2,1)}, u32[]{:S(2)}) copy-start(bf16[2560]{0:T(1024)(128)(2,1)} %param.15) | copy-start | bytes 15364
  7.2 109.5 %copy-start.7 = (s32[4096]{0:T(1024)S(1)}, s32[4096]{0:T(1024)}, u32[]{:S(2)}) copy-start(s32[4096]{0:T(1024)} %param.17) | copy-start | bytes 49156
  10.2 118.3 %copy-start.6 = (s32[128,6]{0,1:T(8,128)S(1)}, s32[128,6]{0,1:T(8,128)}, u32[]{:S(2)}) copy-start(s32[128,6]{0,1:T(8,128)} %param.12) | copy-start | bytes 9220
  14.3 70.4 %all-to-all-start = ((bf16[32,1,16,2560]{3,2,1,0:T(8,128)(2,1)}), bf16[32,1,16,2560]{3,2,1,0:T(8,128)(2,1)}, u32[]{:S(2)}, u32[]{:S(2)}) async-start(bf16[32,1,16,2560]{3,2,1,0:T(8,128)(2,1)} %fusion.3), calls=%async_computation | async-start | bytes 5242880 | tf_op jit(solution)/shard_map/all_to_all | solution.py:87
  24.6 138.4 %copy-start.2 = (bf16[160,1664]{1,0:T(8,128)(2,1)S(1)}, bf16[160,1664]{1,0:T(8,128)(2,1)}, u32[]{:S(2)}) copy-start(bf16[160,1664]{1,0:T(8,128)(2,1)} %param.16) | copy-start | bytes 1597444
  24.6 15.1 %collective-permute-start = (bf16[160,1664]{1,0:T(8,128)(2,1)}, bf16[160,1664]{1,0:T(8,128)(2,1)S(1)}, u32[]{:S(2)}, u32[]{:S(2)}) collective-permute-start(bf16[160,1664]{1,0:T(8,128)(2,1)} %param.16), channel_id=1, source_target_pairs={{0,1},{1,2},{2,3},{3,4},{4,5},{5,6},{6,7},{7,8},{8,9},{9,10},{10,1... | collective-permute-start | bytes 1597448 | tf_op jit(solution)/shard_map/ppermute | solution.py:16
  39.8 0.8 copy-start.3
  40.6 9.9 %collective-permute-start.1 = (bf16[160,1664]{1,0:T(8,128)(2,1)S(1)}, bf16[160,1664]{1,0:T(8,128)(2,1)S(1)}, u32[]{:S(2)}, u32[]{:S(2)}) collective-permute-start(bf16[160,1664]{1,0:T(8,128)(2,1)S(1)} %collective-permute-done), channel_id=1, source_target_pairs={{0,1},{1,2},{2,3},{3,4},{4,5},{5,6},{6,7},{7,8},{8,9},{9,10},{10,1... | collective-permute-start | bytes 1597448 | tf_op jit(solution)/shard_map/ppermute | solution.py:16
  40.6 10.7 %collective-permute-start.8 = (bf16[160,1664]{1,0:T(8,128)(2,1)}, bf16[160,1664]{1,0:T(8,128)(2,1)}, u32[]{:S(2)}, u32[]{:S(2)}) collective-permute-start(bf16[160,1664]{1,0:T(8,128)(2,1)} %param.16), channel_id=1, source_target_pairs={{0,15},{1,0},{2,1},{3,2},{4,3},{5,4},{6,5},{7,6},{8,7},{9,8},{10,9... | collective-permute-start | bytes 1597448 | tf_op jit(solution)/shard_map/ppermute | solution.py:18
  50.5 0.8 copy-start.4
  51.3 10.0 %collective-permute-start.2 = (bf16[160,1664]{1,0:T(8,128)(2,1)S(1)}, bf16[160,1664]{1,0:T(8,128)(2,1)}, u32[]{:S(2)}, u32[]{:S(2)}) collective-permute-start(bf16[160,1664]{1,0:T(8,128)(2,1)S(1)} %collective-permute-done.1), channel_id=1, source_target_pairs={{0,1},{1,2},{2,3},{3,4},{4,5},{5,6},{6,7},{7,8},{8,9},{9,10},{10,1... | collective-permute-start | bytes 1597448 | tf_op jit(solution)/shard_map/ppermute | solution.py:16
  51.3 47.7 %collective-permute-start.9 = (bf16[160,1664]{1,0:T(8,128)(2,1)}, bf16[160,1664]{1,0:T(8,128)(2,1)}, u32[]{:S(2)}, u32[]{:S(2)}) collective-permute-start(bf16[160,1664]{1,0:T(8,128)(2,1)} %collective-permute-done.8), channel_id=1, source_target_pairs={{0,15},{1,0},{2,1},{3,2},{4,3},{5,4},{6,5},{7,6},{8,7},{9,8},{10,9... | collective-permute-start | bytes 1597448 | tf_op jit(solution)/shard_map/ppermute | solution.py:18
  61.3 44.8 %collective-permute-start.3 = (bf16[160,1664]{1,0:T(8,128)(2,1)}, bf16[160,1664]{1,0:T(8,128)(2,1)}, u32[]{:S(2)}, u32[]{:S(2)}) collective-permute-start(bf16[160,1664]{1,0:T(8,128)(2,1)} %collective-permute-done.2), channel_id=1, source_target_pairs={{0,1},{1,2},{2,3},{3,4},{4,5},{5,6},{6,7},{7,8},{8,9},{9,10},{10,1... | collective-permute-start | bytes 1597448 | tf_op jit(solution)/shard_map/ppermute | solution.py:16
  91.6 74.2 %all-to-all-start.1 = ((bf16[32,1,16,2560]{3,2,1,0:T(8,128)(2,1)}), bf16[32,1,16,2560]{3,2,1,0:T(8,128)(2,1)}, u32[]{:S(2)}, u32[]{:S(2)}) async-start(bf16[32,1,16,2560]{3,2,1,0:T(8,128)(2,1)} %fusion.2), calls=%async_computation.1 | async-start | bytes 5242880 | tf_op jit(solution)/shard_map/all_to_all | solution.py:95
  98.9 129.9 %reduce-scatter.2.cloned.1.call-start = ((), (), s32[]{:S(2)}) async-start(), calls=%async_computation.3 | async-start | bytes 1392640 | tf_op jit(solution)/shard_map/reduce_scatter | solution.py:99
  99.0 14.2 %collective-permute-start.10 = (bf16[160,1664]{1,0:T(8,128)(2,1)}, bf16[160,1664]{1,0:T(8,128)(2,1)}, u32[]{:S(2)}, u32[]{:S(2)}) collective-permute-start(bf16[160,1664]{1,0:T(8,128)(2,1)} %collective-permute-done.9), channel_id=1, source_target_pairs={{0,15},{1,0},{2,1},{3,2},{4,3},{5,4},{6,5},{7,6},{8,7},{9,8},{10,9... | collective-permute-start | bytes 1597448 | tf_op jit(solution)/shard_map/ppermute | solution.py:18
  106.1 10.5 %collective-permute-start.4 = (bf16[160,1664]{1,0:T(8,128)(2,1)}, bf16[160,1664]{1,0:T(8,128)(2,1)}, u32[]{:S(2)}, u32[]{:S(2)}) collective-permute-start(bf16[160,1664]{1,0:T(8,128)(2,1)} %collective-permute-done.3), channel_id=1, source_target_pairs={{0,1},{1,2},{2,3},{3,4},{4,5},{5,6},{6,7},{7,8},{8,9},{9,10},{10,1... | collective-permute-start | bytes 1597448 | tf_op jit(solution)/shard_map/ppermute | solution.py:16
  113.2 10.5 %collective-permute-start.11 = (bf16[160,1664]{1,0:T(8,128)(2,1)}, bf16[160,1664]{1,0:T(8,128)(2,1)}, u32[]{:S(2)}, u32[]{:S(2)}) collective-permute-start(bf16[160,1664]{1,0:T(8,128)(2,1)} %collective-permute-done.10), channel_id=1, source_target_pairs={{0,15},{1,0},{2,1},{3,2},{4,3},{5,4},{6,5},{7,6},{8,7},{9,8},{10,9... | collective-permute-start | bytes 1597448 | tf_op jit(solution)/shard_map/ppermute | solution.py:18
  116.6 10.5 %collective-permute-start.5 = (bf16[160,1664]{1,0:T(8,128)(2,1)}, bf16[160,1664]{1,0:T(8,128)(2,1)}, u32[]{:S(2)}, u32[]{:S(2)}) collective-permute-start(bf16[160,1664]{1,0:T(8,128)(2,1)} %collective-permute-done.4), channel_id=1, source_target_pairs={{0,1},{1,2},{2,3},{3,4},{4,5},{5,6},{6,7},{7,8},{8,9},{9,10},{10,1... | collective-permute-start | bytes 1597448 | tf_op jit(solution)/shard_map/ppermute | solution.py:16
  123.7 10.5 %collective-permute-start.12 = (bf16[160,1664]{1,0:T(8,128)(2,1)}, bf16[160,1664]{1,0:T(8,128)(2,1)}, u32[]{:S(2)}, u32[]{:S(2)}) collective-permute-start(bf16[160,1664]{1,0:T(8,128)(2,1)} %collective-permute-done.11), channel_id=1, source_target_pairs={{0,15},{1,0},{2,1},{3,2},{4,3},{5,4},{6,5},{7,6},{8,7},{9,8},{10,9... | collective-permute-start | bytes 1597448 | tf_op jit(solution)/shard_map/ppermute | solution.py:18
  127.1 10.5 %collective-permute-start.6 = (bf16[160,1664]{1,0:T(8,128)(2,1)}, bf16[160,1664]{1,0:T(8,128)(2,1)}, u32[]{:S(2)}, u32[]{:S(2)}) collective-permute-start(bf16[160,1664]{1,0:T(8,128)(2,1)} %collective-permute-done.5), channel_id=1, source_target_pairs={{0,1},{1,2},{2,3},{3,4},{4,5},{5,6},{6,7},{7,8},{8,9},{9,10},{10,1... | collective-permute-start | bytes 1597448 | tf_op jit(solution)/shard_map/ppermute | solution.py:16
  134.2 10.5 %collective-permute-start.13 = (bf16[160,1664]{1,0:T(8,128)(2,1)}, bf16[160,1664]{1,0:T(8,128)(2,1)}, u32[]{:S(2)}, u32[]{:S(2)}) collective-permute-start(bf16[160,1664]{1,0:T(8,128)(2,1)} %collective-permute-done.12), channel_id=1, source_target_pairs={{0,15},{1,0},{2,1},{3,2},{4,3},{5,4},{6,5},{7,6},{8,7},{9,8},{10,9... | collective-permute-start | bytes 1597448 | tf_op jit(solution)/shard_map/ppermute | solution.py:18
  137.7 10.5 %collective-permute-start.7 = (bf16[160,1664]{1,0:T(8,128)(2,1)}, bf16[160,1664]{1,0:T(8,128)(2,1)S(1)}, u32[]{:S(2)}, u32[]{:S(2)}) collective-permute-start(bf16[160,1664]{1,0:T(8,128)(2,1)} %collective-permute-done.6), channel_id=1, source_target_pairs={{0,1},{1,2},{2,3},{3,4},{4,5},{5,6},{6,7},{7,8},{8,9},{9,10},{10,1... | collective-permute-start | bytes 1597448 | tf_op jit(solution)/shard_map/ppermute | solution.py:16
  144.8 35.1 %collective-permute-start.14 = (bf16[160,1664]{1,0:T(8,128)(2,1)}, bf16[160,1664]{1,0:T(8,128)(2,1)}, u32[]{:S(2)}, u32[]{:S(2)}) collective-permute-start(bf16[160,1664]{1,0:T(8,128)(2,1)} %collective-permute-done.13), channel_id=1, source_target_pairs={{0,15},{1,0},{2,1},{3,2},{4,3},{5,4},{6,5},{7,6},{8,7},{9,8},{10,9... | collective-permute-start | bytes 1597448 | tf_op jit(solution)/shard_map/ppermute | solution.py:18
  148.2 0.9 copy-start.5
  170.3 140.4 %all-gather.2.cloned.1.call-start = ((), (), s32[]{:S(2)}) async-start(), calls=%async_computation.4 | async-start | bytes 1351680 | tf_op jit(solution)/shard_map/all_gather | solution.py:103
Sparse Core Ops, SparseCore 0:
  170.4 58.3 reduce-scatter.1
  232.0 78.6 all-gather.1
